TPU v7x, 32 devices: a whole 2x2x4 slice. The times are simulated.
32 devices in a mesh: groups: 2 (over x), branch: 2 (over core), sub: 8 (over z, y).
Axes of the slice: x: 2, y: 2, z: 4, core: 2. Of those that a mesh axis runs over, the one named last changes fastest.
Arguments:
- dispatch: float32 [128, 168, 2048], P(('groups', 'branch', 'sub')), parts along dimension 0, may hold values from 0 to 3
- multiplier: float32 [128, 48, 2048], P(('groups', 'branch', 'sub')), parts along dimension 0, may hold values from -3 to 3
- node_of: int32 [128], P(('groups', 'branch', 'sub')), parts along dimension 0, may hold values from 0 to 7, as said below
- prob_weight: int32 [128], P(('groups', 'branch', 'sub')), parts along dimension 0, may hold values from 1 to 16
- commitment: int32 [128, 168, 2048], P(('groups', 'branch', 'sub')), parts along dimension 0, may hold values 0 or 1
- zone_of: int32 [2048], replicated, may hold values from 0 to 31
- capacity: float32 [2048], replicated, may hold values from 0.5 to 4
- linear_cost: float32 [2048], replicated, may hold values from -0.5 to 1
- quad_cost: float32 [2048], replicated, may hold values from 0.5 to 2
- demand: float32 [128, 168, 32], P(('groups', 'branch', 'sub')), parts along dimension 0, may hold values from 19 to 64
Outputs:
- new_dispatch: float32 [128, 168, 2048], P(('groups', 'branch', 'sub')), parts along dimension 0
- new_multiplier: float32 [128, 48, 2048], P(('groups', 'branch', 'sub')), parts along dimension 0
- next_average: float32 [128, 48, 2048], P(('groups', 'branch', 'sub')), parts along dimension 0
- deviation: float32 [2], P('groups'), parts along dimension 0
There are 2 independent parts, one for each index of `groups`. A program takes and returns all parts, laid end to end along the dimension named above; an argument that names none is the same for every part. Nothing has to cross between parts.
Inputs may be any that keep to these rules, and one draw needn't show every extreme that they name: `node_of`: within each aligned block of 32 scenarios (one day-one branch), every node number holds exactly 4 scenarios.
All inputs are finite; a program needn't handle non-finite values. No bound on the sum of `commitment` on one device may be relied on, other than what follows from the above.
Results may differ from a plain program's by a relative error of at most 0.0001.
Values sent between devices are 32-bit elements; how exact they have to be, the bound alone decides.
A program may use at most 128 MiB of HBM per device.

v0:
```python
import jax
import jax.numpy as jnp
from jax import lax
from jax.sharding import PartitionSpec as P

DAY = 24
NODES_BR = 8
STEPS = 3
rho_value = 1.0
step_size = 0.3


def average(early_part, prob_weight, node_of, riding):
    weighting = prob_weight.astype(jnp.float32)
    scen_local = early_part.shape[0]
    gens = early_part.shape[2]
    member = (node_of[None, :] == jnp.arange(NODES_BR, dtype=jnp.int32)[:, None]).astype(
        jnp.float32
    )
    weighted = member * weighting[None, :]
    day_one = jnp.einsum(
        "s,stg->tg", weighting, early_part[:, :DAY], precision=lax.Precision.HIGHEST
    )
    weight_sum = jnp.sum(weighting)[None]
    day_two = jnp.einsum(
        "ks,stg->ktg", weighted, early_part[:, DAY:], precision=lax.Precision.HIGHEST
    )
    node_weight = jnp.sum(weighted, axis=1)
    day_two, node_weight = lax.psum((day_two, node_weight), "sub")
    day_one, weight_sum, riding = lax.psum((day_one, weight_sum, riding), ("branch", "sub"))
    root_mean = day_one / weight_sum[0]
    node_mean = day_two / node_weight[:, None, None]
    assigned = jnp.einsum("ks,ktg->stg", member, node_mean, precision=lax.Precision.HIGHEST)
    spread_root = jnp.broadcast_to(root_mean[None], (scen_local, DAY, gens))
    return (jnp.concatenate([spread_root, assigned], axis=1), weight_sum, riding)


def shards(
    dispatch,
    multiplier,
    node_of,
    prob_weight,
    commitment,
    zone_of,
    capacity,
    linear_cost,
    quad_cost,
    demand,
):
    section_hours = multiplier.shape[1]
    gens = zone_of.shape[0]
    zones_count = demand.shape[2]
    weighting = prob_weight.astype(jnp.float32)
    nothing = jnp.zeros((1,), jnp.float32)
    averages, weight_sum, unused = average(
        dispatch[:, :section_hours], prob_weight, node_of, nothing
    )
    spread_gap = dispatch[:, :section_hours] - averages
    local_spread = jnp.sum(weighting[:, None, None] * spread_gap * spread_gap)[None]
    dev_total = lax.psum(local_spread, ("branch", "sub"))
    new_multiplier = multiplier + rho_value * spread_gap
    zone_table = (zone_of[:, None] == jnp.arange(zones_count, dtype=jnp.int32)[None, :]).astype(
        jnp.float32
    )
    ceiling = capacity[None, None, :] * commitment.astype(jnp.float32)
    balance = zones_count / gens
    current = dispatch
    for sweep in range(STEPS):
        zone_sum = jnp.einsum("stg,gz->stz", current, zone_table, precision=lax.Precision.HIGHEST)
        mismatch = zone_sum - demand
        feedback = jnp.einsum("stz,gz->stg", mismatch, zone_table, precision=lax.Precision.HIGHEST)
        gradient = linear_cost + quad_cost * current + balance * feedback
        hedged = (
            gradient[:, :section_hours]
            + new_multiplier
            + rho_value * (current[:, :section_hours] - averages)
        )
        gradient = jnp.concatenate([hedged, gradient[:, section_hours:]], axis=1)
        current = jnp.clip(current - step_size * gradient, 0.0, ceiling)
    next_average, unused_sum, carried = average(
        current[:, :section_hours], prob_weight, node_of, nothing
    )
    deviation = dev_total / (weight_sum * section_hours * gens)
    return (current, new_multiplier, next_average, deviation)


def solution(mesh):
    in_specs = (
        P(("groups", "branch", "sub"), None, None),
        P(("groups", "branch", "sub"), None, None),
        P(("groups", "branch", "sub")),
        P(("groups", "branch", "sub")),
        P(("groups", "branch", "sub"), None, None),
        P(),
        P(),
        P(),
        P(),
        P(("groups", "branch", "sub"), None, None),
    )
    out_specs = (
        P(("groups", "branch", "sub"), None, None),
        P(("groups", "branch", "sub"), None, None),
        P(("groups", "branch", "sub"), None, None),
        P("groups"),
    )
    return jax.shard_map(shards, mesh=mesh, in_specs=in_specs, out_specs=out_specs, check_vma=False)
```

profile of v0, /device:TPU:0, one launch (start us, length us, event | category | flops | bytes accessed | tf_op | source)
XLA Modules:
  0.0 428.4 jit_solution(12756518674870253161)
XLA Ops:
  8.8 2.5 fusion.25
  12.7 4.0 fusion.23
  17.5 35.9 %psum.56 = f32[1]{0:T(128)} all-reduce(f32[1]{0:T(128)} %bitcast.4), channel_id=1, replica_groups=mesh['groups'=2,'branch'=2,'sub'=8] {'branch','sub'}, use_global_device_ids=true, to_apply=%region_2.0 | all-reduce | flops 1 | bytes 8 | tf_op jit(solution)/shard_map/psum | solution.py:30
  53.4 17.6 %psum.58 = f32[8]{0:T(128)S(1)} all-reduce(f32[8]{0:T(128)S(1)} %select_reduce_fusion), channel_id=1, replica_groups=mesh['groups'=2,'branch'=2,'sub'=8] {'sub'}, use_global_device_ids=true, to_apply=%region_5.0 | all-reduce | flops 8 | bytes 64 | tf_op jit(solution)/shard_map/psum | solution.py:29
  71.1 5.7 %fusion.18 = f32[4,168,32]{1,2,0:T(8,128)S(1)} fusion(f32[4,168,32]{1,2,0:T(8,128)S(1)} %copy-done.6, f32[4,168,2048]{2,1,0:T(8,128)} %param.10, s32[2048]{0:T(1024)S(1)} %copy-done.7), kind=kOutput, calls=%fused_computation.36 | convolution fusion | flops 528569344 | bytes 5685248 | tf_op jit(solution)/shard_map/stg,gz->stz/dot_general | solution.py:69
  76.8 3.0 multiply_add_fusion.2
  79.8 2.4 copy-done.1
  82.2 22.3 %all-reduce.5.cloned.1.call-done = f32[24,2048]{1,0:T(8,128)} async-done(((f32[24,2048]{1,0:T(8,128)}), f32[24,2048]{1,0:T(8,128)}) %all-reduce.5.cloned.1.call-update) | async-done | bytes 196624 | tf_op jit(solution)/shard_map/psum | solution.py:30
  106.1 90.5 %all-reduce.7.cloned.1.call-done = f32[8,24,2048]{2,0,1:T(8,128)} async-done(((f32[8,24,2048]{2,0,1:T(8,128)}), f32[8,24,2048]{2,0,1:T(8,128)}) %all-reduce.7.cloned.1.call-update) | async-done | bytes 1572880 | tf_op jit(solution)/shard_map/psum | solution.py:29
  196.5 2.5 fusion.16
  199.7 2.9 fusion.12
  204.0 4.0 fusion.2
  208.0 3.0 convolution_subtract_fusion.1
  211.0 3.0 multiply_add_fusion.1
  216.7 2.9 fusion.5
  219.6 3.0 convolution_subtract_fusion
  222.6 3.0 multiply_add_fusion
  226.4 2.6 fusion.8
  229.1 2.4 copy-done.4
  234.3 3.3 fusion.19
  238.3 32.6 %psum.61 = f32[1]{0:T(128)} all-reduce(f32[1]{0:T(128)} %bitcast.10), channel_id=1, replica_groups=mesh['groups'=2,'branch'=2,'sub'=8] {'branch','sub'}, use_global_device_ids=true, to_apply=%region_9.10 | all-reduce | flops 1 | bytes 8 | tf_op jit(solution)/shard_map/psum | solution.py:60
  271.5 52.0 %all-reduce.9.cloned.1.call-done = f32[24,2048]{1,0:T(8,128)} async-done(((f32[24,2048]{1,0:T(8,128)}), f32[24,2048]{1,0:T(8,128)}) %all-reduce.9.cloned.1.call-update) | async-done | bytes 196624 | tf_op jit(solution)/shard_map/psum | solution.py:30
  325.1 90.3 %all-reduce.11.cloned.1.call-done = f32[8,24,2048]{2,0,1:T(8,128)} async-done(((f32[8,24,2048]{2,0,1:T(8,128)}), f32[8,24,2048]{2,0,1:T(8,128)}) %all-reduce.11.cloned.1.call-update) | async-done | bytes 1572880 | tf_op jit(solution)/shard_map/psum | solution.py:29
  415.4 2.4 fusion.14
  (63 shorter events, 18.2 us)
Async XLA Ops:
  7.2 9.6 %copy-start.11 = (s32[4]{0:T(128)S(1)}, s32[4]{0:T(128)}, u32[]{:S(2)}) copy-start(s32[4]{0:T(128)} %param.13) | copy-start | bytes 52
  7.2 10.2 %copy-start.12 = (s32[4]{0:T(128)S(1)}, s32[4]{0:T(128)}, u32[]{:S(2)}) copy-start(s32[4]{0:T(128)} %param.12) | copy-start | bytes 52
  7.2 63.9 %copy-start.7 = (s32[2048]{0:T(1024)S(1)}, s32[2048]{0:T(1024)}, u32[]{:S(2)}) copy-start(s32[2048]{0:T(1024)} %param.15) | copy-start | bytes 24580
  7.2 63.8 %copy-start.6 = (f32[4,168,32]{1,2,0:T(8,128)S(1)}, f32[4,168,32]{1,2,0:T(8,128)}, u32[]{:S(2)}) copy-start(f32[4,168,32]{1,2,0:T(8,128)} %param.19) | copy-start | bytes 258052
  7.2 97.3 %all-reduce.5.cloned.1.call-start = ((), (), s32[]{:S(2)}) async-start(), calls=%async_computation | async-start | bytes 393216 | tf_op jit(solution)/shard_map/psum | solution.py:30
  8.8 68.0 %copy-start.9 = (f32[2048]{0:T(1024)S(1)}, f32[2048]{0:T(1024)}, u32[]{:S(2)}) copy-start(f32[2048]{0:T(1024)} %param.18) | copy-start | bytes 24580
  8.8 68.0 %copy-start.10 = (f32[2048]{0:T(1024)S(1)}, f32[2048]{0:T(1024)}, u32[]{:S(2)}) copy-start(f32[2048]{0:T(1024)} %param.17) | copy-start | bytes 24580
  12.0 184.5 %all-reduce.7.cloned.1.call-start = ((), (), s32[]{:S(2)}) async-start(), calls=%async_computation.1 | async-start | bytes 3145728 | tf_op jit(solution)/shard_map/psum | solution.py:29
  16.7 306.8 %all-reduce.9.cloned.1.call-start = ((), (), s32[]{:S(2)}) async-start(), calls=%async_computation.2 | async-start | bytes 393216 | tf_op jit(solution)/shard_map/psum | solution.py:30
  71.0 5.7 %copy-start = (f32[4,168,2048]{2,1,0:T(8,128)S(1)}, f32[4,168,2048]{2,1,0:T(8,128)}, u32[]{:S(2)}) copy-start(f32[4,168,2048]{2,1,0:T(8,128)} %param.10) | copy-start | bytes 16515076
  79.8 2.4 copy-start.1
  82.2 117.4 %copy-start.5 = (f32[4,48,2048]{2,1,0:T(8,128)S(1)}, f32[4,48,2048]{2,1,0:T(8,128)}, u32[]{:S(2)}) copy-start(f32[4,48,2048]{2,1,0:T(8,128)} %param.11) | copy-start | bytes 4718596
  196.5 3.1 copy-start.2
  199.5 3.0 slice-start
  199.5 3.8 slice-start.4
  199.5 3.8 copy-start.8
  199.6 4.4 %slice-start.1 = ((s8[5505024]{0:T(1024)(128)(4,1)}), s8[1310720]{0:T(1024)(128)(4,1)S(1)}, s32[]{:S(2)}) async-start(s8[5505024]{0:T(1024)(128)(4,1)} %bitcast.41), calls=%async_computation.5 | async-start | bytes 2621440
  202.5 23.1 %copy-start.3 = (f32[4,48,2048]{2,1,0:T(8,128)}, f32[4,48,2048]{2,1,0:T(8,128)S(1)}, u32[]{:S(2)}) copy-start(f32[4,48,2048]{2,1,0:T(8,128)S(1)} %get-tuple-element.9) | copy-start | bytes 4718596
  214.0 2.2 slice-start.2
  214.5 2.2 slice-start.3
  229.1 2.4 copy-start.4
  234.3 181.1 %all-reduce.11.cloned.1.call-start = ((), (), s32[]{:S(2)}) async-start(), calls=%async_computation.3 | async-start | bytes 3145728 | tf_op jit(solution)/shard_map/psum | solution.py:29
Sparse Core Ops, SparseCore 0:
  12.1 92.3 all-reduce.4
  108.6 87.8 all-reduce.6
  234.4 89.0 all-reduce.8
  327.5 87.8 all-reduce.10
where the time goes:
time: 429 us; the launch traced here: 428 us
  waiting for transfers between devices  255 us (59%)
  blocking collectives  86.1 us (20%)
  matrix products  37.2 us (9%)
  other arithmetic  18.6 us (4%)
  between operations  16.5 us (4%)
  local copies, waits for them, and re-layouts  14.7 us (3%)
    psum x2, waiting for transfers between devices, average(): day_two, node_weight = lax.psum((day_two, node_weight), 'sub')  181 us
    psum x2, waiting for transfers between devices, average(): lax.psum((day_one, weight_sum, riding), ('branch', 'sub'))  74.3 us
    psum x1, blocking collectives, average(): lax.psum((day_one, weight_sum, riding), ('branch', 'sub'))  35.9 us
    psum x1, blocking collectives, shards(): dev_total = lax.psum(local_spread, ('branch', 'sub'))  32.6 us
    psum x1, blocking collectives, average(): day_two, node_weight = lax.psum((day_two, node_weight), 'sub')  17.6 us
    dot_general x3, matrix products, shards(): jnp.einsum('stg,gz->stz', current, zone_table, precision=lax.Precision.HI...  11.6 us
    min x3, other arithmetic, shards(): current = jnp.clip(current - step_size * gradient, 0.0, ceiling)  9.51 us
    unnamed x35, local copies, waits for them, and re-layouts  9.42 us
  transfers between devices with their start and end apart: 4, of which 4 were waited for; matrix products, arithmetic and copies ran while one was open for 5% of the time, Pallas kernels for 0%

commit v1 on v0

--- a/solution.py
+++ b/solution.py
@@ -57,7 +57,7 @@
     )
     spread_gap = dispatch[:, :section_hours] - averages
     local_spread = jnp.sum(weighting[:, None, None] * spread_gap * spread_gap)[None]
-    dev_total = lax.psum(local_spread, ("branch", "sub"))
+    dev_total = jnp.sum(lax.all_gather(local_spread, ("branch", "sub")), axis=0)
     new_multiplier = multiplier + rho_value * spread_gap
     zone_table = (zone_of[:, None] == jnp.arange(zones_count, dtype=jnp.int32)[None, :]).astype(
         jnp.float32

time: 429 us -> 429 us (level)
    psum x1 -> x0, blocking collectives: 32.6 us -> none  [shards(): dev_total = lax.psum(local_spread, ('branch', 'sub'))]
    unnamed x0 -> x1, blocking collectives: none -> 31.9 us
    unnamed x35 -> x40, local copies, waits for them, and re-layouts: 9.42 us -> 11.4 us
where the time goes in v1:
time: 429 us
  waiting for transfers between devices  253 us (59%)
  blocking collectives  85.4 us (20%)
  matrix products  37.2 us (9%)
  other arithmetic  19.1 us (4%)
  local copies, waits for them, and re-layouts  16.7 us (4%)
  between operations  16.5 us (4%)
    psum x2, waiting for transfers between devices, average(): day_two, node_weight = lax.psum((day_two, node_weight), 'sub')  181 us
    psum x2, waiting for transfers between devices, average(): lax.psum((day_one, weight_sum, riding), ('branch', 'sub'))  72.5 us
    psum x1, blocking collectives, average(): lax.psum((day_one, weight_sum, riding), ('branch', 'sub'))  35.9 us
    unnamed x1, blocking collectives  31.9 us
    psum x1, blocking collectives, average(): day_two, node_weight = lax.psum((day_two, node_weight), 'sub')  17.6 us
    dot_general x3, matrix products, shards(): jnp.einsum('stg,gz->stz', current, zone_table, precision=lax.Precision.HI...  11.6 us
    unnamed x40, local copies, waits for them, and re-layouts  11.4 us
    min x3, other arithmetic, shards(): current = jnp.clip(current - step_size * gradient, 0.0, ceiling)  9.51 us
  transfers between devices with their start and end apart: 4, of which 4 were waited for; matrix products, arithmetic and copies ran while one was open for 5% of the time, Pallas kernels for 0%

profile of v1, /device:TPU:0, one launch (start us, length us, event | category | flops | bytes accessed | tf_op | source)
XLA Modules:
  0.0 428.5 jit_solution(8918878337972799002)
XLA Ops:
  8.8 2.5 fusion.25
  12.7 4.0 fusion.23
  17.5 35.9 %psum.49 = f32[1]{0:T(128)} all-reduce(f32[1]{0:T(128)} %bitcast.4), channel_id=1, replica_groups=mesh['groups'=2,'branch'=2,'sub'=8] {'branch','sub'}, use_global_device_ids=true, to_apply=%region_2.0 | all-reduce | flops 1 | bytes 8 | tf_op jit(solution)/shard_map/psum | solution.py:30
  53.4 17.6 %psum.51 = f32[8]{0:T(128)S(1)} all-reduce(f32[8]{0:T(128)S(1)} %select_reduce_fusion), channel_id=1, replica_groups=mesh['groups'=2,'branch'=2,'sub'=8] {'sub'}, use_global_device_ids=true, to_apply=%region_5.0 | all-reduce | flops 8 | bytes 64 | tf_op jit(solution)/shard_map/psum | solution.py:29
  71.0 5.7 %fusion.18 = f32[4,168,32]{1,2,0:T(8,128)S(1)} fusion(f32[4,168,32]{1,2,0:T(8,128)S(1)} %copy-done.6, f32[4,168,2048]{2,1,0:T(8,128)} %param.10, s32[2048]{0:T(1024)S(1)} %copy-done.7), kind=kOutput, calls=%fused_computation.36 | convolution fusion | flops 528569344 | bytes 5685248 | tf_op jit(solution)/shard_map/stg,gz->stz/dot_general | solution.py:69
  76.7 3.0 multiply_add_fusion.2
  79.7 2.4 copy-done.1
  82.2 22.3 %all-reduce.6.cloned.1.call-done = f32[24,2048]{1,0:T(8,128)} async-done(((f32[24,2048]{1,0:T(8,128)}), f32[24,2048]{1,0:T(8,128)}) %all-reduce.6.cloned.1.call-update) | async-done | bytes 196624 | tf_op jit(solution)/shard_map/psum | solution.py:30
  106.0 90.5 %all-reduce.8.cloned.1.call-done = f32[8,24,2048]{2,0,1:T(8,128)} async-done(((f32[8,24,2048]{2,0,1:T(8,128)}), f32[8,24,2048]{2,0,1:T(8,128)}) %all-reduce.8.cloned.1.call-update) | async-done | bytes 1572880 | tf_op jit(solution)/shard_map/psum | solution.py:29
  196.6 2.5 fusion.16
  199.7 2.9 fusion.12
  204.1 4.0 fusion.2
  208.1 3.0 convolution_subtract_fusion.1
  211.1 3.0 multiply_add_fusion.1
  216.8 2.9 fusion.5
  219.6 3.0 convolution_subtract_fusion
  222.6 3.0 multiply_add_fusion
  226.5 2.6 fusion.8
  229.1 2.4 copy-done.4
  234.4 3.3 fusion.19
  240.3 31.9 %all-reduce = f32[16]{0:T(128)S(1)} all-reduce(f32[16]{0:T(128)S(1)} %dynamic-update-slice), channel_id=1, replica_groups=mesh['groups'=2,'branch'=2,'sub'=8] {'branch','sub'}, use_global_device_ids=true, to_apply=%add | all-reduce | flops 16 | bytes 128
  273.5 50.2 %all-reduce.10.cloned.1.call-done = f32[24,2048]{1,0:T(8,128)} async-done(((f32[24,2048]{1,0:T(8,128)}), f32[24,2048]{1,0:T(8,128)}) %all-reduce.10.cloned.1.call-update) | async-done | bytes 196624 | tf_op jit(solution)/shard_map/psum | solution.py:30
  325.1 90.4 %all-reduce.12.cloned.1.call-done = f32[8,24,2048]{2,0,1:T(8,128)} async-done(((f32[8,24,2048]{2,0,1:T(8,128)}), f32[8,24,2048]{2,0,1:T(8,128)}) %all-reduce.12.cloned.1.call-update) | async-done | bytes 1572880 | tf_op jit(solution)/shard_map/psum | solution.py:29
  415.5 2.4 fusion.14
  (69 shorter events, 20.7 us)
Async XLA Ops:
  7.2 9.6 %copy-start.11 = (s32[4]{0:T(128)S(1)}, s32[4]{0:T(128)}, u32[]{:S(2)}) copy-start(s32[4]{0:T(128)} %param.13) | copy-start | bytes 52
  7.2 10.2 %copy-start.12 = (s32[4]{0:T(128)S(1)}, s32[4]{0:T(128)}, u32[]{:S(2)}) copy-start(s32[4]{0:T(128)} %param.12) | copy-start | bytes 52
  7.2 63.8 %copy-start.7 = (s32[2048]{0:T(1024)S(1)}, s32[2048]{0:T(1024)}, u32[]{:S(2)}) copy-start(s32[2048]{0:T(1024)} %param.15) | copy-start | bytes 24580
  7.2 63.8 %copy-start.6 = (f32[4,168,32]{1,2,0:T(8,128)S(1)}, f32[4,168,32]{1,2,0:T(8,128)}, u32[]{:S(2)}) copy-start(f32[4,168,32]{1,2,0:T(8,128)} %param.19) | copy-start | bytes 258052
  7.2 97.3 %all-reduce.6.cloned.1.call-start = ((), (), s32[]{:S(2)}) async-start(), calls=%async_computation | async-start | bytes 393216 | tf_op jit(solution)/shard_map/psum | solution.py:30
  8.8 67.9 %copy-start.9 = (f32[2048]{0:T(1024)S(1)}, f32[2048]{0:T(1024)}, u32[]{:S(2)}) copy-start(f32[2048]{0:T(1024)} %param.18) | copy-start | bytes 24580
  8.8 67.9 %copy-start.10 = (f32[2048]{0:T(1024)S(1)}, f32[2048]{0:T(1024)}, u32[]{:S(2)}) copy-start(f32[2048]{0:T(1024)} %param.17) | copy-start | bytes 24580
  12.0 184.5 %all-reduce.8.cloned.1.call-start = ((), (), s32[]{:S(2)}) async-start(), calls=%async_computation.1 | async-start | bytes 3145728 | tf_op jit(solution)/shard_map/psum | solution.py:29
  16.7 306.9 %all-reduce.10.cloned.1.call-start = ((), (), s32[]{:S(2)}) async-start(), calls=%async_computation.2 | async-start | bytes 393216 | tf_op jit(solution)/shard_map/psum | solution.py:30
  71.0 5.7 %copy-start = (f32[4,168,2048]{2,1,0:T(8,128)S(1)}, f32[4,168,2048]{2,1,0:T(8,128)}, u32[]{:S(2)}) copy-start(f32[4,168,2048]{2,1,0:T(8,128)} %param.10) | copy-start | bytes 16515076
  79.7 2.4 copy-start.1
  82.2 117.5 %copy-start.5 = (f32[4,48,2048]{2,1,0:T(8,128)S(1)}, f32[4,48,2048]{2,1,0:T(8,128)}, u32[]{:S(2)}) copy-start(f32[4,48,2048]{2,1,0:T(8,128)} %param.11) | copy-start | bytes 4718596
  196.6 3.1 copy-start.2
  199.5 3.0 slice-start
  199.5 3.8 slice-start.4
  199.6 3.8 copy-start.8
  199.7 4.4 %slice-start.1 = ((s8[5505024]{0:T(1024)(128)(4,1)}), s8[1310720]{0:T(1024)(128)(4,1)S(1)}, s32[]{:S(2)}) async-start(s8[5505024]{0:T(1024)(128)(4,1)} %bitcast.43), calls=%async_computation.5 | async-start | bytes 2621440
  202.5 23.1 %copy-start.3 = (f32[4,48,2048]{2,1,0:T(8,128)}, f32[4,48,2048]{2,1,0:T(8,128)S(1)}, u32[]{:S(2)}) copy-start(f32[4,48,2048]{2,1,0:T(8,128)S(1)} %get-tuple-element.9) | copy-start | bytes 4718596
  214.1 2.2 slice-start.2
  214.5 2.2 slice-start.3
  229.1 2.4 copy-start.4
  231.5 6.2 %copy-start.13 = (u32[32]{0:T(128)S(1)}, u32[32]{0:T(128)}, u32[]{:S(2)}) copy-start(u32[32]{0:T(128)} %constant.19) | copy-start | bytes 388
  234.3 181.2 %all-reduce.12.cloned.1.call-start = ((), (), s32[]{:S(2)}) async-start(), calls=%async_computation.3 | async-start | bytes 3145728 | tf_op jit(solution)/shard_map/psum | solution.py:29
Sparse Core Ops, SparseCore 0:
  12.1 92.3 all-reduce.5
  108.6 87.8 all-reduce.7
  234.5 89.1 all-reduce.9
  327.6 87.8 all-reduce.11
